TPU v7x, 256 devices: a whole 4x4x8 slice. The times are simulated.
256 devices in a mesh: kv: 4 (over y), seq: 64 (over z, x, core).
Axes of the slice: x: 4, y: 4, z: 8, core: 2. Of those that a mesh axis runs over, the one named last changes fastest.
Arguments:
- sampled_rows: int32 [6144], replicated, may hold values from 0 to 16383, as said below
- query_vectors: bfloat16 [6144, 64, 128], P('seq', 'kv'), may hold values from -150 to 150
- key_vectors: bfloat16 [16384, 8, 128], P('seq', 'kv'), may hold values from -6 to 6
Outputs:
- heavy_hitters: float32 [16384], P('seq')
Inputs may be any that keep to these rules, and one draw needn't show every extreme that they name: `sampled_rows`: strictly increasing sequence positions.
All inputs are finite; a program needn't handle non-finite values.
Results may differ from a plain program's by a relative error of at most 0.0003.
Values may be sent and summed in bfloat16 or wider, within the bound.
A program may use at most 64 MiB of HBM per device.

v0:
```python
import math
import jax
import jax.numpy as jnp
from jax import lax
from jax.sharding import PartitionSpec as P

HD = 128
NEG = -1e30


def split_up(array, dim, devices):
    before, after = (array.shape[:dim], array.shape[dim + 1 :])
    return jnp.moveaxis(array.reshape(*before, devices, -1, *after), dim, 0)


def sum_at_owner(array, axis, dim):
    devices = lax.axis_size(axis)
    tiles = lax.all_to_all(split_up(array, dim, devices), axis, 0, 0, tiled=True)
    return jnp.sum(tiles, axis=0)


def copy_for_each(array, axis):
    copies = jnp.broadcast_to(array, (lax.axis_size(axis), *array.shape))
    return lax.all_to_all(copies, axis, split_axis=0, concat_axis=0, tiled=True)


def of_everyone(array, axis):
    return copy_for_each(array, axis).sum(axis=0)


def block_scores(query_block, key_block, factor):
    return (
        jnp.einsum("rgid,kgd->rgik", query_block, key_block, preferred_element_type=jnp.float32)
        * factor
    )


def visibility(rows_block, offset, amount):
    places = offset + jnp.arange(amount, dtype=jnp.int32)
    return places[None, None, None, :] <= rows_block[:, None, None, None]


def stats_block(query_block, rows_block, key_block, offset, running, factor):
    row_max, row_total = running
    scores = block_scores(query_block, key_block, factor)
    visible = visibility(rows_block, offset, key_block.shape[0])
    scores = jnp.where(visible, scores, NEG)
    new_max = jnp.maximum(row_max, jnp.max(scores, axis=-1))
    terms = jnp.where(visible, jnp.exp(scores - new_max[..., None]), 0.0)
    return (new_max, row_total * jnp.exp(row_max - new_max) + jnp.sum(terms, axis=-1))


def prob_columns(query_block, rows_block, key_block, offset, log_total, factor):
    scores = block_scores(query_block, key_block, factor)
    visible = visibility(rows_block, offset, key_block.shape[0])
    probability = jnp.where(visible, jnp.exp(scores - log_total[..., None]), 0.0)
    return jnp.sum(probability, axis=(0, 1, 2))


def on_device(sampled_rows, query_vectors, key_vectors):
    local_rows = query_vectors.shape[0]
    local_keys = key_vectors.shape[0]
    local_groups = key_vectors.shape[1]
    group_size = query_vectors.shape[1] // local_groups
    factor = 1.0 / math.sqrt(HD)
    seq_index = lax.axis_index("seq")
    grouped = query_vectors.reshape(local_rows, local_groups, group_size, HD)
    own_rows = lax.dynamic_slice_in_dim(sampled_rows, seq_index * local_rows, local_rows, 0)
    highest = jnp.max(own_rows)
    gathered = lax.all_gather(key_vectors, "seq", axis=0, tiled=True)
    total_keys = gathered.shape[0]
    key_stride = math.gcd(total_keys, 2048)

    def sweep(running, key_index):
        offset = key_index * key_stride

        def sweep_active(state):
            key_block = lax.dynamic_slice_in_dim(gathered, offset, key_stride, 0)
            return stats_block(grouped, own_rows, key_block, offset, state, factor)

        return (lax.cond(offset <= highest, sweep_active, lambda state: state, running), None)

    initial = (
        jnp.full((local_rows, local_groups, group_size), NEG, jnp.float32),
        jnp.zeros((local_rows, local_groups, group_size), jnp.float32),
    )
    (row_max, row_total), _ = lax.scan(
        sweep, initial, jnp.arange(total_keys // key_stride, dtype=jnp.int32)
    )
    log_total = row_max + jnp.log(row_total)

    def terms(offset, amount):
        stride = math.gcd(amount, 2048)

        def portion(block_index):
            first = block_index * stride

            def portion_active():
                key_block = lax.dynamic_slice_in_dim(gathered, first, stride, 0)
                return prob_columns(grouped, own_rows, key_block, first, log_total, factor)

            return lax.cond(
                first <= highest, portion_active, lambda: jnp.zeros((stride,), jnp.float32)
            )

        return lax.map(portion, jnp.arange(amount // stride, dtype=jnp.int32)).reshape(amount)

    columns = sum_at_owner(terms(jnp.int32(0), local_keys * lax.axis_size("seq")), "seq", 0)
    summed = of_everyone(columns, "kv")
    return summed * (1.0 / group_size)


def solution(mesh):
    placed = (P(), P("seq", "kv", None), P("seq", "kv", None))
    return jax.shard_map(on_device, mesh=mesh, in_specs=placed, out_specs=P("seq"), check_vma=False)
```

profile of v0, /device:TPU:1, one launch (start us, length us, event | category | flops | bytes accessed | tf_op | source)
XLA Modules:
  0.0 263.4 jit_solution(13679895400350161696)
XLA Ops:
  6.5 1.6 copy.10
  8.2 1.1 copy.11
  9.3 1.5 fusion.11
  10.7 86.6 %all-gather.2.cloned.1.call-done = bf16[16384,2,128]{2,0,1:T(8,128)(2,1)} async-done(((bf16[256,2,128]{2,0,1:T(8,128)(2,1)}), bf16[16384,2,128]{2,0,1:T(8,128)(2,1)}) %all-gather.2.cloned.1.call-update) | async-done | bytes 8388624 | tf_op jit(solution)/shard_map/all_gather | solution.py:70
  97.4 22.9 %while.22 = (s32[]{:T(128)}, f32[96,2,8]{0,2,1:T(8,128)S(1)}, f32[96,2,8]{0,2,1:T(8,128)S(1)}, s32[8]{0:T(128)S(1)}, s32[]{:T(128)}, /*index=5*/s32[96]{0:T(128)...) while((s32[]{:T(128)}, f32[96,2,8]{0,2,1:T(8,128)S(1)}, ...), condition=%wide.region_6.7_spmd, body=%wide.region_1.6_spmd.sunk | while | flops 830673920 | bytes 27294348 | solution.py:87
  97.4 0.6 dynamic_slice.30
  99.3 7.4 %conditional.4 = ((f32[96,2,8]{0,2,1:T(8,128)S(1)}, f32[96,2,8]{0,2,1:T(8,128)S(1)})) conditional(s32[]{:T(128)} %convert_element_type.8, (f32[96,2,8]{0,2,1:T(8,128)S(1)}, f32[96,2,8]{0,2,1:T(8,128)S(1)}) %tuple.51, (s32[]{:T(128)}, s32[96]{0:T(128)S(1)}, bf16[16384,2,128]{2,0,1:T(8,128)(2,1)}, bf16[96,2,8,128]{3,0,2,1:T(8,128)(2,1)S(1)}, ...), branch_computations={%region_2.2_spmd, %region_3.5_spmd} | conditional | flops 830673920 | bytes 27294146 | solution.py:81
  99.5 3.7 %fusion = (f32[96,2,8]{0,2,1:T(8,128)S(1)}, f32[2,2048,96,8]{1,2,3,0:T(8,128)S(1)}) fusion(pred[96,2048]{1,0:T(8,128)(4,1)S(1)} %broadcast_compare_fusion, bf16[96,2,8,128]{3,0,2,1:T(8,128)(2,1)S(1)} %get-tuple-element.103, bf16[16384,2,128]{2,0,1:T(8,128)(2,1)} %get-tuple-element.102, s32[]{:T(128)S(6)} %select_n.13), kind=kOutput, calls=%fused_computation.2 | convolution fusion | flops 814742016 | bytes 14227460 | tf_op jit(solution)/shard_map/while/body/eval_jaxpr/cond/branch_1_fun/rgid,kgd->rgik/dot_general | solution.py:33
  103.1 3.5 %select_reduce_fusion = f32[96,2,8]{0,2,1:T(8,128)S(1)} fusion(f32[2,2048,96,8]{1,2,3,0:T(8,128)S(1)} %get-tuple-element.171, f32[96,2,8]{0,2,1:T(8,128)S(1)} %max.2, pred[96,2048]{1,0:T(8,128)(4,1)S(1)} %broadcast_compare_fusion), kind=kLoop, calls=%fused_computation.1 | loop fusion | flops 15727104 | bytes 12791808 | tf_op jit(solution)/shard_map/while/body/eval_jaxpr/cond/branch_1_fun/reduce_sum | solution.py:50
  106.7 0.6 dynamic_slice.30
  108.7 0.6 dynamic_slice.30
  110.6 0.6 dynamic_slice.30
  112.5 0.6 dynamic_slice.30
  114.5 0.6 dynamic_slice.30
  116.4 0.6 dynamic_slice.30
  118.4 0.6 dynamic_slice.30
  120.3 22.7 %while.23 = (s32[]{:T(128)}, f32[8,2048]{1,0:T(8,128)S(1)}, s32[8]{0:T(128)S(1)}, s32[]{:T(128)}, s32[96]{0:T(128)S(1)}, /*index=5*/bf16[16384,2,128]{2,0,1:T(8,...) while((s32[]{:T(128)}, f32[8,2048]{1,0:T(8,128)S(1)}, ...), condition=%wide.region_11.12_spmd, body=%wide.region_7.11_spmd.sunk | while | flops 818085888 | bytes 1882737 | solution.py:106
  120.3 0.6 dynamic_slice.31
  122.2 5.4 %conditional.5 = (f32[1,2048]{1,0:T(1,128)S(1)}) conditional(s32[]{:T(128)} %convert_element_type.9, () %tuple.54, (s32[]{:T(128)}, s32[96]{0:T(128)S(1)}, bf16[16384,2,128]{2,0,1:T(8,128)(2,1)}, bf16[96,2,8,128]{3,0,2,1:T(8,128)(2,1)S(1)}, f32[96,2,8]{0,2,1:T(8,128)S(1)}) %tuple.55), branch_computations={%region_8.8_spmd, %region_9.10_spmd} | conditional | flops 818085888 | bytes 1866162 | solution.py:102
  122.5 5.1 %fusion.7 = f32[2048]{0:T(1024)S(1)} fusion(f32[96,2,8]{0,2,1:T(8,128)S(1)} %get-tuple-element.120, pred[96,2048]{1,0:T(8,128)(4,1)S(1)} %broadcast_compare_fusion.1, bf16[96,2,8,128]{3,0,2,1:T(8,128)(2,1)S(1)} %get-tuple-element.119, bf16[16384,2,128]{2,0,1:T(8,128)(2,1)} %get-tuple-element.118, s32[]{:T(128)S(6)} %select_n.16), kind=kOutput, calls=%fused_computation.13 | convolution fusion | flops 817887232 | bytes 1652740 | tf_op jit(solution)/shard_map/while/body/eval_jaxpr/cond/branch_1_fun/rgid,kgd->rgik/dot_general | solution.py:33
  127.6 0.2 dynamic_update_slice.5
  127.8 0.6 dynamic_slice.31
  129.8 0.2 dynamic_update_slice.5
  130.0 0.6 dynamic_slice.31
  132.2 0.6 dynamic_slice.31
  134.3 0.6 dynamic_slice.31
  136.5 0.6 dynamic_slice.31
  138.7 0.6 dynamic_slice.31
  140.8 0.6 dynamic_slice.31
  143.1 104.8 %all_to_all.15 = f32[64,1,256]{2,1,0:T(1,128)S(1)} all-to-all(f32[64,1,256]{2,1,0:T(1,128)S(1)} %all_to_all.10), channel_id=1, replica_groups=mesh['kv'=4,'seq'=64] {'seq'}, dimensions={0} | all-to-all | bytes 131072 | tf_op jit(solution)/shard_map/all_to_all | solution.py:18
  248.0 8.0 %all_to_all.16 = f32[4,1,256]{2,1,0:T(1,128)S(1)} all-to-all(f32[4,1,256]{2,1,0:T(1,128)S(1)} %broadcast_in_dim.55), channel_id=1, replica_groups=mesh['kv'=4,'seq'=64] {'kv'}, dimensions={0} | all-to-all | bytes 8192 | tf_op jit(solution)/shard_map/all_to_all | solution.py:24
  256.0 0.6 broadcast_multiply_fusion
  (46 shorter events, 2.1 us)
Async XLA Ops:
  6.5 90.8 %all-gather.2.cloned.1.call-start = ((), (), s32[]{:S(2)}) async-start(), calls=%async_computation.2 | async-start | bytes 8519680 | tf_op jit(solution)/shard_map/all_gather | solution.py:70
Sparse Core Ops, SparseCore 0:
  10.2 87.1 all-gather.1
where the time goes:
time: 265 us; the launch traced here: 263 us
  blocking collectives  113 us (43%)
  waiting for transfers between devices  86.6 us (33%)
  loops' own time  21.6 us (8%)
  local copies, waits for them, and re-layouts  14 us (5%)
  between operations  13.5 us (5%)
  matrix products  8.79 us (3%)
  other arithmetic  6.1 us (2%)
    all_to_all x1, blocking collectives, sum_at_owner(): lax.all_to_all(split_up(array, dim, devices), axis, 0, 0, tiled=True)  105 us
    all_gather x1, waiting for transfers between devices, on_device(): gathered = lax.all_gather(key_vectors, 'seq', axis=0, tiled=True)  86.6 us
    another operation x1, loops' own time, terms(): lax.map(portion, jnp.arange(amount // stride, dtype=jnp.int32))  10.7 us
    another operation x1, loops' own time, on_device(): lax.scan(sweep, initial, jnp.arange(total_keys // key_stride, dtype=jnp.i...  10.6 us
    dynamic_slice x16, local copies, waits for them, and re-layouts, on_device(): lax.scan(sweep, initial, jnp.arange(total_keys // key_stride, dtype=jnp.i...  9.59 us
    dot_general x2, matrix products, block_scores(): jnp.einsum('rgid,kgd->rgik', query_block, key_block, preferred_element_ty...  8.79 us
    all_to_all x1, blocking collectives, copy_for_each(): return lax.all_to_all(copies, axis, split_axis=0, concat_axis=0, tiled=True)  7.96 us
  transfers between devices with their start and end apart: 1, of which 1 were waited for; matrix products, arithmetic and copies ran while one was open for 1% of the time, Pallas kernels for 0%

commit v1 on v0

--- a/solution.py
+++ b/solution.py
@@ -67,7 +67,10 @@
     grouped = query_vectors.reshape(local_rows, local_groups, group_size, HD)
     own_rows = lax.dynamic_slice_in_dim(sampled_rows, seq_index * local_rows, local_rows, 0)
     highest = jnp.max(own_rows)
-    gathered = lax.all_gather(key_vectors, "seq", axis=0, tiled=True)
+    size = lax.axis_size("seq")
+    shards = jnp.stack([key_vectors for _ in range(size)])
+    shards = lax.all_to_all(shards, "seq", split_axis=0, concat_axis=0)
+    gathered = jnp.concatenate(shards, axis=0)
     total_keys = gathered.shape[0]
     key_stride = math.gcd(total_keys, 2048)
 

time: 265 us -> 372 us (1.40)
  waiting for transfers between devices: 86.6 us -> 181 us
  between operations: 13.5 us -> 0.1 us
  starting transfers between devices: 0.01 us -> 13.2 us
  local copies, waits for them, and re-layouts: 14 us -> 25.4 us
    all_to_all x0 -> x1, waiting for transfers between devices: none -> 181 us  [on_device(): shards = lax.all_to_all(shards, 'seq', split_axis=0, concat_axis=0)]
    all_gather x1 -> x0, waiting for transfers between devices: 86.6 us -> none  [on_device(): gathered = lax.all_gather(key_vectors, 'seq', axis=0, tiled=True)]
    all_to_all x0 -> x1, starting transfers between devices: none -> 13.2 us  [on_device(): shards = lax.all_to_all(shards, 'seq', split_axis=0, concat_axis=0)]
    all_to_all x0 -> x1, local copies, waits for them, and re-layouts: none -> 7.71 us  [on_device(): shards = lax.all_to_all(shards, 'seq', split_axis=0, concat_axis=0)]
    another operation x0 -> x1, local copies, waits for them, and re-layouts: none -> 5.31 us  [on_device(): shards = jnp.stack([key_vectors for _ in range(size)])]
  transfers between devices with their start and end apart: 1 -> 1, of which waited for: 1 -> 1; matrix products, arithmetic and copies ran while one was open for 1% -> 0% of each run, Pallas kernels for 0% -> 0%
where the time goes in v1:
time: 372 us; the launch traced here: 370 us
  waiting for transfers between devices  181 us (49%)
  blocking collectives  116 us (31%)
  local copies, waits for them, and re-layouts  25.4 us (7%)
  loops' own time  19.8 us (5%)
  starting transfers between devices  13.2 us (4%)
  matrix products  8.79 us (2%)
  other arithmetic  6.03 us (2%)
    all_to_all x1, waiting for transfers between devices, on_device(): shards = lax.all_to_all(shards, 'seq', split_axis=0, concat_axis=0)  181 us
    all_to_all x1, blocking collectives, sum_at_owner(): lax.all_to_all(split_up(array, dim, devices), axis, 0, 0, tiled=True)  108 us
    all_to_all x1, starting transfers between devices, on_device(): shards = lax.all_to_all(shards, 'seq', split_axis=0, concat_axis=0)  13.2 us
    another operation x1, loops' own time, terms(): lax.map(portion, jnp.arange(amount // stride, dtype=jnp.int32))  9.8 us
    another operation x1, loops' own time, on_device(): lax.scan(sweep, initial, jnp.arange(total_keys // key_stride, dtype=jnp.i...  9.73 us
    dynamic_slice x16, local copies, waits for them, and re-layouts, on_device(): lax.scan(sweep, initial, jnp.arange(total_keys // key_stride, dtype=jnp.i...  9.59 us
    dot_general x2, matrix products, block_scores(): jnp.einsum('rgid,kgd->rgik', query_block, key_block, preferred_element_ty...  8.79 us
    all_to_all x1, blocking collectives, copy_for_each(): return lax.all_to_all(copies, axis, split_axis=0, concat_axis=0, tiled=True)  8.12 us
  transfers between devices with their start and end apart: 1, of which 1 were waited for; matrix products, arithmetic and copies ran while one was open for 0% of the time, Pallas kernels for 0%

profile of v1, /device:TPU:1, one launch (start us, length us, event | category | flops | bytes accessed | tf_op | source)
XLA Modules:
  0.0 370.5 jit_solution(15703312049944045497)
XLA Ops:
  0.0 0.9 copy.14
  0.9 5.3 %stack.2 = bf16[64,256,2,128]{3,1,2,0:T(8,128)(2,1)} broadcast(bf16[256,2,128]{2,0,1:T(8,128)(2,1)S(1)} %copy.14), dimensions={1,2,3} | broadcast | bytes 8519680 | tf_op jit(solution)/shard_map/stack | solution.py:71
  6.3 13.2 %all-to-all-start = ((bf16[64,256,2,128]{3,1,2,0:T(8,128)(2,1)}), bf16[64,256,2,128]{3,1,2,0:T(8,128)(2,1)}, u32[]{:S(2)}, u32[]{:S(2)}) async-start(bf16[64,256,2,128]{3,1,2,0:T(8,128)(2,1)} %stack.2), calls=%async_computation | async-start | bytes 16777216 | tf_op jit(solution)/shard_map/all_to_all | solution.py:72
  19.6 1.4 fusion.11
  21.0 180.8 %all-to-all-done = bf16[64,256,2,128]{3,1,2,0:T(8,128)(2,1)} async-done(((bf16[64,256,2,128]{3,1,2,0:T(8,128)(2,1)}), bf16[64,256,2,128]{3,1,2,0:T(8,128)(2,1)}, u32[]{:S(2)}, u32[]{:S(2)}) %all-to-all-start) | async-done | bytes 8388640 | tf_op jit(solution)/shard_map/all_to_all | solution.py:72
  201.8 7.7 %copy.15 = bf16[64,256,2,128]{3,1,0,2:T(8,128)(2,1)} copy(bf16[64,256,2,128]{3,1,2,0:T(8,128)(2,1)} %all-to-all-done) | data formatting | bytes 16777216 | tf_op jit(solution)/shard_map/all_to_all | solution.py:72
  209.5 22.0 %while.22 = (s32[]{:T(128)}, f32[96,2,8]{0,2,1:T(8,128)S(1)}, f32[96,2,8]{0,2,1:T(8,128)S(1)}, s32[8]{0:T(128)S(1)}, s32[]{:T(128)}, /*index=5*/s32[96]{0:T(128)...) while((s32[]{:T(128)}, f32[96,2,8]{0,2,1:T(8,128)S(1)}, ...), condition=%wide.region_6.7_spmd, body=%wide.region_1.6_spmd.sunk | while | flops 830673920 | bytes 27294348 | solution.py:90
  209.5 0.6 dynamic_slice.30
  211.3 7.5 %conditional.4 = ((f32[96,2,8]{0,2,1:T(8,128)S(1)}, f32[96,2,8]{0,2,1:T(8,128)S(1)})) conditional(s32[]{:T(128)} %convert_element_type.8, (f32[96,2,8]{0,2,1:T(8,128)S(1)}, f32[96,2,8]{0,2,1:T(8,128)S(1)}) %tuple.51, (s32[]{:T(128)}, s32[96]{0:T(128)S(1)}, bf16[16384,2,128]{2,0,1:T(8,128)(2,1)}, bf16[96,2,8,128]{3,0,2,1:T(8,128)(2,1)S(1)}, ...), branch_computations={%region_2.2_spmd, %region_3.5_spmd} | conditional | flops 830673920 | bytes 27294146 | solution.py:84
  211.5 3.7 fusion
  215.2 3.5 select_reduce_fusion
  218.8 0.6 dynamic_slice.30
  220.6 0.6 dynamic_slice.30
  222.5 0.6 dynamic_slice.30
  224.3 0.6 dynamic_slice.30
  226.1 0.6 dynamic_slice.30
  227.9 0.6 dynamic_slice.30
  229.8 0.6 dynamic_slice.30
  231.6 21.8 %while.23 = (s32[]{:T(128)}, f32[8,2048]{1,0:T(8,128)S(1)}, s32[8]{0:T(128)S(1)}, s32[]{:T(128)}, s32[96]{0:T(128)S(1)}, /*index=5*/bf16[16384,2,128]{2,0,1:T(8,...) while((s32[]{:T(128)}, f32[8,2048]{1,0:T(8,128)S(1)}, ...), condition=%wide.region_11.12_spmd, body=%wide.region_7.11_spmd.sunk | while | flops 818085888 | bytes 1882737 | solution.py:109
  231.6 0.6 dynamic_slice.31
  233.4 5.4 %conditional.5 = (f32[1,2048]{1,0:T(1,128)S(1)}) conditional(s32[]{:T(128)} %convert_element_type.9, () %tuple.54, (s32[]{:T(128)}, s32[96]{0:T(128)S(1)}, bf16[16384,2,128]{2,0,1:T(8,128)(2,1)}, bf16[96,2,8,128]{3,0,2,1:T(8,128)(2,1)S(1)}, f32[96,2,8]{0,2,1:T(8,128)S(1)}) %tuple.55), branch_computations={%region_8.8_spmd, %region_9.10_spmd} | conditional | flops 818085888 | bytes 1866162 | solution.py:105
  233.6 5.1 %fusion.7 = f32[2048]{0:T(1024)S(1)} fusion(f32[96,2,8]{0,2,1:T(8,128)S(1)} %get-tuple-element.120, pred[96,2048]{1,0:T(8,128)(4,1)S(1)} %broadcast_compare_fusion.1, bf16[96,2,8,128]{3,0,2,1:T(8,128)(2,1)S(1)} %get-tuple-element.119, bf16[16384,2,128]{2,0,1:T(8,128)(2,1)} %get-tuple-element.118, s32[]{:T(128)S(6)} %select_n.16), kind=kOutput, calls=%fused_computation.13 | convolution fusion | flops 817887232 | bytes 1652740 | tf_op jit(solution)/shard_map/while/body/eval_jaxpr/cond/branch_1_fun/rgid,kgd->rgik/dot_general | solution.py:33
  239.0 0.6 dynamic_slice.31
  241.1 0.6 dynamic_slice.31
  243.1 0.6 dynamic_slice.31
  245.2 0.6 dynamic_slice.31
  247.2 0.6 dynamic_slice.31
  249.3 0.6 dynamic_slice.31
  251.3 0.6 dynamic_slice.31
  253.5 108.2 %all_to_all.20 = f32[64,1,256]{2,1,0:T(1,128)S(1)} all-to-all(f32[64,1,256]{2,1,0:T(1,128)S(1)} %all_to_all.14), channel_id=1, replica_groups=mesh['kv'=4,'seq'=64] {'seq'}, dimensions={0} | all-to-all | bytes 131072 | tf_op jit(solution)/shard_map/all_to_all | solution.py:18
  361.8 8.1 %all_to_all.21 = f32[4,1,256]{2,1,0:T(1,128)S(1)} all-to-all(f32[4,1,256]{2,1,0:T(1,128)S(1)} %broadcast_in_dim.55), channel_id=1, replica_groups=mesh['kv'=4,'seq'=64] {'kv'}, dimensions={0} | all-to-all | bytes 8192 | tf_op jit(solution)/shard_map/all_to_all | solution.py:24
  369.9 0.6 broadcast_multiply_fusion
  (49 shorter events, 2.6 us)
Async XLA Ops:
  0.9 18.5 %copy-start = (bf16[96,16,128]{2,1,0:T(8,128)(2,1)S(1)}, bf16[96,16,128]{2,1,0:T(8,128)(2,1)}, u32[]{:S(2)}) copy-start(bf16[96,16,128]{2,1,0:T(8,128)(2,1)} %param.12) | copy-start | bytes 1179652
  6.3 195.6 %all-to-all-start = ((bf16[64,256,2,128]{3,1,2,0:T(8,128)(2,1)}), bf16[64,256,2,128]{3,1,2,0:T(8,128)(2,1)}, u32[]{:S(2)}, u32[]{:S(2)}) async-start(bf16[64,256,2,128]{3,1,2,0:T(8,128)(2,1)} %stack.2), calls=%async_computation | async-start | bytes 16777216 | tf_op jit(solution)/shard_map/all_to_all | solution.py:72
